TPU v7x, 32 devices: a whole 2x2x4 slice. The times are simulated.
32 devices in a mesh: rep: 4 (over y, x), shard: 8 (over z, core).
Axes of the slice: x: 2, y: 2, z: 4, core: 2. Of those that a mesh axis runs over, the one named last changes fastest.
Arguments:
- tokens: bfloat16 [8192, 1024], P(('rep', 'shard')), may hold values from -6 to 6
- choices: int32 [8192, 8], P(('rep', 'shard')), may hold values from 0 to 31, all different within a row; in each aligned block of 256 rows (0 to 255, 256 to 511, ...) at most 96 rows name the same one
- cont_lengths: int32 [4, 2], P('rep'), may hold values from 1 to 768, 1024 in all within a row
- norm_attn: bfloat16 [1024], P('shard'), may hold values from 0.5 to 1.5
- w_qkv: bfloat16 [1024, 2048], P('shard'), may hold values from -0.1875 to 0.1875
- w_out: bfloat16 [1024, 1024], P('shard'), may hold values from -1.5 to 1.5
- norm_ffn: bfloat16 [1024], P('shard'), may hold values from 0.5 to 1.5
- w_router: bfloat16 [1024, 32], P('shard'), may hold values from -0.25 to 0.25
- w_gate_up: bfloat16 [32, 1024, 1024], P('shard'), may hold values from -0.1875 to 0.1875
- w_down: bfloat16 [32, 512, 1024], P('shard'), may hold values from -0.25 to 0.25
- cotangent: bfloat16 [8192, 1024], P(('rep', 'shard')), may hold values from -6 to 6
Outputs:
- output: bfloat16 [8192, 1024], P(('rep', 'shard'))
- d_tokens: float32 [8192, 1024], P(('rep', 'shard'))
- grad_norm_attn: float32 [1024], P('shard')
- grad_qkv: float32 [1024, 2048], P('shard')
- grad_out: float32 [1024, 1024], P('shard')
- grad_norm_ffn: float32 [1024], P('shard')
- grad_router: float32 [1024, 32], P('shard')
- grad_gate_up: float32 [32, 1024, 1024], P('shard')
- grad_down: float32 [32, 512, 1024], P('shard')
Inputs may be any that keep to these rules, and one draw needn't show every extreme that they name: `choices`: in the rows of one device (aligned blocks of 256 rows) no expert is named by more than 96 rows, a bound that some block reaches; a row names 8 different experts. `cont_lengths`: each row holds the 2 continuation lengths of one group; they sum to 1024 and none is longer than 768.
All inputs are finite; a program needn't handle non-finite values.
Results may differ from a plain program's by a relative error of at most 0.02.
Values may be sent and summed in bfloat16 or wider, within the bound.
A program may use at most 192 MiB of HBM per device.

v0:
```python
import jax
import jax.numpy as jnp
from jax import lax
from jax.sharding import PartitionSpec as P

HEADS = 16
KV_HEADS = 8
HEAD = 64
EXPERTS = 32
FF = 512
TOPK = 8
CAP = 96
EPSILON = 1e-06


def layout(lengths, tok_index, prompt_len):
    starts = prompt_len + jnp.cumsum(lengths) - lengths
    passed = tok_index[:, None] >= starts[None, :]
    segment = jnp.sum(passed.astype(jnp.int32), axis=1)
    seg_start = jnp.max(jnp.where(passed, starts[None, :], 0), axis=1)
    position = jnp.where(segment > 0, tok_index - seg_start + prompt_len, tok_index)
    return (segment, position)


def rotary(field_rows, position, direction):
    half_width = field_rows.shape[-1] // 2
    freq_table = 10000.0 ** (-jnp.arange(half_width, dtype=jnp.float32) / half_width)
    angle_table = direction * position.astype(jnp.float32)[:, None] * freq_table[None, :]
    cosine = jnp.cos(angle_table)[:, None, :]
    sine_part = jnp.sin(angle_table)[:, None, :]
    first_half = field_rows[..., :half_width]
    second_half = field_rows[..., half_width:]
    return jnp.concatenate(
        [
            first_half * cosine - second_half * sine_part,
            second_half * cosine + first_half * sine_part,
        ],
        axis=-1,
    )


def block_scores(queries, query_index, query_segment, key_rot, key_index, key_segment):
    scores = jnp.einsum(
        "qgrd,kgd->grqk", queries, key_rot, preferred_element_type=jnp.float32
    ) * queries.shape[-1] ** (-0.5)
    allowed = (key_index[None, :] <= query_index[:, None]) & (
        (key_segment[None, :] == 0) | (key_segment[None, :] == query_segment[:, None])
    )
    return (jnp.where(allowed, scores, -1e30), allowed)


def on_device(
    tokens,
    choices,
    cont_lengths,
    norm_attn,
    w_qkv,
    w_out,
    norm_ffn,
    w_router,
    w_gate_up,
    w_down,
    cotangent,
):
    row_count = tokens.shape[0]
    model_width = tokens.shape[1]
    shard_count = lax.axis_size("shard")
    group_len = row_count * shard_count
    prompt_len = group_len // 2
    lengths_row = cont_lengths[0]
    tok_index = lax.axis_index("shard") * row_count + jnp.arange(row_count, dtype=jnp.int32)
    segment, position = layout(lengths_row, tok_index, prompt_len)
    gain_attn, full_qkv, full_out, gain_ffn, full_router = (
        lax.all_gather(norm_attn, "shard", axis=0, tiled=True),
        lax.all_gather(w_qkv, "shard", axis=0, tiled=True),
        lax.all_gather(w_out, "shard", axis=0, tiled=True),
        lax.all_gather(norm_ffn, "shard", axis=0, tiled=True),
        lax.all_gather(w_router, "shard", axis=0, tiled=True),
    )
    gain_attn = gain_attn.astype(jnp.float32)
    gain_ffn = gain_ffn.astype(jnp.float32)
    tokens_f = tokens.astype(jnp.float32)
    inv_one = lax.rsqrt(jnp.mean(tokens_f * tokens_f, axis=1, keepdims=True) + EPSILON)
    normed_one = tokens_f * inv_one
    first_in = (normed_one * gain_attn).astype(jnp.bfloat16)
    qkv_rows = jnp.dot(first_in, full_qkv, preferred_element_type=jnp.float32)
    query_width = HEADS * HEAD
    key_width = KV_HEADS * HEAD
    repeat_count = HEADS // KV_HEADS
    score_scale = HEAD ** (-0.5)
    queries = (
        rotary(qkv_rows[:, :query_width].reshape(row_count, HEADS, HEAD), position, 1.0)
        .astype(jnp.bfloat16)
        .reshape(row_count, KV_HEADS, repeat_count, HEAD)
    )
    key_rot = rotary(
        qkv_rows[:, query_width : query_width + key_width].reshape(row_count, KV_HEADS, HEAD),
        position,
        1.0,
    ).astype(jnp.bfloat16)
    values = (
        qkv_rows[:, query_width + key_width :]
        .astype(jnp.bfloat16)
        .reshape(row_count, KV_HEADS, HEAD)
    )
    all_keys, all_values = (
        lax.all_gather(key_rot, "shard", axis=0, tiled=True),
        lax.all_gather(values, "shard", axis=0, tiled=True),
    )
    key_block = min(512, prompt_len)
    blocks = group_len // key_block
    group_index = jnp.arange(group_len, dtype=jnp.int32)
    group_segment, group_position = layout(lengths_row, group_index, prompt_len)
    key_stack = (
        all_keys.reshape(blocks, key_block, KV_HEADS, HEAD),
        all_values.reshape(blocks, key_block, KV_HEADS, HEAD),
        group_index.reshape(blocks, key_block),
        group_segment.reshape(blocks, key_block),
    )
    stat_shape = (KV_HEADS, repeat_count, row_count)

    def stats_step(state_acc, key_piece):
        run_max, run_sum = state_acc
        scores, allowed = block_scores(
            queries, tok_index, segment, key_piece[0], key_piece[2], key_piece[3]
        )
        new_max = jnp.maximum(run_max, jnp.max(scores, axis=-1))
        run_sum = run_sum * jnp.exp(run_max - new_max) + jnp.sum(
            jnp.where(allowed, jnp.exp(scores - new_max[..., None]), 0.0), axis=-1
        )
        return ((new_max, run_sum), None)

    (run_max, run_sum), unused = lax.scan(
        stats_step,
        (jnp.full(stat_shape, -1e30, jnp.float32), jnp.zeros(stat_shape, jnp.float32)),
        key_stack,
    )
    log_total = run_max + jnp.log(run_sum)

    def prob_block(key_piece):
        scores, allowed = block_scores(
            queries, tok_index, segment, key_piece[0], key_piece[2], key_piece[3]
        )
        return jnp.where(allowed, jnp.exp(scores - log_total[..., None]), 0.0)

    def mix_step(total_mix, key_piece):
        prob_f32 = prob_block(key_piece)
        return (
            total_mix
            + jnp.einsum(
                "grqk,kgd->qgrd",
                prob_f32.astype(jnp.bfloat16),
                key_piece[1],
                preferred_element_type=jnp.float32,
            ),
            None,
        )

    mix_f32, unused = lax.scan(
        mix_step, jnp.zeros((row_count, KV_HEADS, repeat_count, HEAD), jnp.float32), key_stack
    )
    mixed_heads = mix_f32.reshape(row_count, query_width).astype(jnp.bfloat16)
    residual = tokens_f + jnp.dot(mixed_heads, full_out, preferred_element_type=jnp.float32)
    inv_two = lax.rsqrt(jnp.mean(residual * residual, axis=1, keepdims=True) + EPSILON)
    normed_two = residual * inv_two
    second_in = (normed_two * gain_ffn).astype(jnp.bfloat16)
    logits = jnp.dot(second_in, full_router, preferred_element_type=jnp.float32)
    expert_ids = jnp.arange(EXPERTS, dtype=jnp.int32)
    select = (choices[:, :, None] == expert_ids[None, None, :]).astype(jnp.float32)
    chosen = jnp.sum(select * logits[:, None, :], axis=2)
    gate_weights = jax.nn.softmax(chosen, axis=-1)
    local_experts = w_down.shape[0]
    flat_choice = choices.reshape(-1)
    pair_count = flat_choice.shape[0]
    onehot = (flat_choice[:, None] == expert_ids[None, :]).astype(jnp.int32)
    slot_rank = jnp.sum((jnp.cumsum(onehot, axis=0) - onehot) * onehot, axis=1)
    slot_place = (
        flat_choice // local_experts * CAP + slot_rank
    ) * local_experts + flat_choice % local_experts
    slot_pair = (
        jnp.full((EXPERTS * CAP,), pair_count, jnp.int32)
        .at[slot_place]
        .set(jnp.arange(pair_count, dtype=jnp.int32))
    )
    padded = jnp.concatenate([second_in, jnp.zeros((1, model_width), jnp.bfloat16)], axis=0)
    send_rows = padded[slot_pair // TOPK].reshape(shard_count, CAP, local_experts, model_width)
    received = lax.all_to_all(send_rows, "shard", split_axis=0, concat_axis=0, tiled=True)
    gate_up = jnp.einsum("nced,edf->ncef", received, w_gate_up, preferred_element_type=jnp.float32)
    hidden = (jax.nn.silu(gate_up[..., :FF]) * gate_up[..., FF:]).astype(jnp.bfloat16)
    expert_out = jnp.einsum(
        "ncef,efd->nced", hidden, w_down, preferred_element_type=jnp.float32
    ).astype(jnp.bfloat16)
    returned = lax.all_to_all(expert_out, "shard", split_axis=0, concat_axis=0, tiled=True).reshape(
        -1, model_width
    )
    pair_out = returned[slot_place].reshape(row_count, TOPK, model_width).astype(jnp.float32)
    output = (residual + jnp.sum(gate_weights[:, :, None] * pair_out, axis=1)).astype(jnp.bfloat16)
    grad_in = cotangent.astype(jnp.float32)
    d_gates = jnp.sum(pair_out * grad_in[:, None, :], axis=2)
    d_pairs = (
        (gate_weights[:, :, None] * grad_in[:, None, :])
        .astype(jnp.bfloat16)
        .reshape(pair_count, model_width)
    )
    d_padded = jnp.concatenate([d_pairs, jnp.zeros((1, model_width), jnp.bfloat16)], axis=0)
    d_send = d_padded[slot_pair].reshape(shard_count, CAP, local_experts, model_width)
    d_received = lax.all_to_all(d_send, "shard", split_axis=0, concat_axis=0, tiled=True)
    gate_up = jnp.einsum("nced,edf->ncef", received, w_gate_up, preferred_element_type=jnp.float32)
    gate_part = gate_up[..., :FF]
    up_part = gate_up[..., FF:]
    sigmoid_gate = jax.nn.sigmoid(gate_part)
    silu_gate = gate_part * sigmoid_gate
    hidden = (silu_gate * up_part).astype(jnp.bfloat16)
    d_hidden = jnp.einsum("nced,efd->ncef", d_received, w_down, preferred_element_type=jnp.float32)
    d_gate_up = jnp.concatenate(
        [
            d_hidden * up_part * sigmoid_gate * (1.0 + gate_part * (1.0 - sigmoid_gate)),
            d_hidden * silu_gate,
        ],
        axis=-1,
    ).astype(jnp.bfloat16)
    grad_down = jnp.einsum("ncef,nced->efd", hidden, d_received, preferred_element_type=jnp.float32)
    grad_gate_up = jnp.einsum(
        "nced,ncef->edf", received, d_gate_up, preferred_element_type=jnp.float32
    )
    d_slots = jnp.einsum(
        "ncef,edf->nced", d_gate_up, w_gate_up, preferred_element_type=jnp.float32
    ).astype(jnp.bfloat16)
    d_back = lax.all_to_all(d_slots, "shard", split_axis=0, concat_axis=0, tiled=True).reshape(
        -1, model_width
    )
    d_second = jnp.sum(
        d_back[slot_place].reshape(row_count, TOPK, model_width).astype(jnp.float32), axis=1
    )
    d_chosen = gate_weights * (d_gates - jnp.sum(gate_weights * d_gates, axis=1, keepdims=True))
    d_logits = jnp.sum(select * d_chosen[:, :, None], axis=1)
    d_second = d_second + jnp.dot(
        d_logits, full_router.astype(jnp.float32).T, precision=lax.Precision.HIGHEST
    )
    grad_router = jnp.dot(
        second_in.astype(jnp.float32).T, d_logits, precision=lax.Precision.HIGHEST
    )
    d_norm_two = d_second * gain_ffn
    grad_ffn = jnp.sum(d_second * normed_two, axis=0)
    d_residual = grad_in + inv_two * (
        d_norm_two - normed_two * jnp.mean(d_norm_two * normed_two, axis=1, keepdims=True)
    )
    d_attn = d_residual.astype(jnp.bfloat16)
    grad_out = jnp.dot(mixed_heads.T, d_attn, preferred_element_type=jnp.float32)
    d_mixed = (
        jnp.dot(d_attn, full_out.T, preferred_element_type=jnp.float32)
        .astype(jnp.bfloat16)
        .reshape(row_count, KV_HEADS, repeat_count, HEAD)
    )

    def delta_step(total_delta, key_piece):
        prob_f32 = prob_block(key_piece)
        d_prob = jnp.einsum(
            "qgrd,kgd->grqk", d_mixed, key_piece[1], preferred_element_type=jnp.float32
        )
        return (total_delta + jnp.sum(prob_f32 * d_prob, axis=-1), None)

    row_delta, unused = lax.scan(delta_step, jnp.zeros(stat_shape, jnp.float32), key_stack)

    def score_grad(key_piece):
        prob_f32 = prob_block(key_piece)
        d_prob = jnp.einsum(
            "qgrd,kgd->grqk", d_mixed, key_piece[1], preferred_element_type=jnp.float32
        )
        return (prob_f32, (prob_f32 * (d_prob - row_delta[..., None])).astype(jnp.bfloat16))

    query_zeros = jnp.zeros((row_count, KV_HEADS, repeat_count, HEAD), jnp.float32)

    def full_step(d_queries, key_piece):
        prob_f32, d_scores = score_grad(key_piece)
        d_queries = (
            d_queries
            + jnp.einsum(
                "grqk,kgd->qgrd", d_scores, key_piece[0], preferred_element_type=jnp.float32
            )
            * score_scale
        )
        key_term = (
            jnp.einsum("grqk,qgrd->kgd", d_scores, queries, preferred_element_type=jnp.float32)
            * score_scale
        )
        value_term = jnp.einsum(
            "grqk,qgrd->kgd",
            prob_f32.astype(jnp.bfloat16),
            d_mixed,
            preferred_element_type=jnp.float32,
        )
        return (d_queries, (key_term, value_term))

    d_queries, block_terms = lax.scan(full_step, query_zeros, key_stack)
    key_terms = block_terms[0].reshape(group_len, key_width)
    value_terms = block_terms[1].reshape(group_len, key_width)
    d_keys, d_values = (
        lax.psum_scatter(
            key_terms.astype(jnp.bfloat16), "shard", scatter_dimension=0, tiled=True
        ).astype(jnp.float32),
        lax.psum_scatter(
            value_terms.astype(jnp.bfloat16), "shard", scatter_dimension=0, tiled=True
        ).astype(jnp.float32),
    )
    d_keys = d_keys.reshape(row_count, KV_HEADS, HEAD)
    d_values = d_values.reshape(row_count, KV_HEADS, HEAD)
    d_query_rows = rotary(d_queries.reshape(row_count, HEADS, HEAD), position, -1.0).reshape(
        row_count, query_width
    )
    d_key_rows = rotary(d_keys, position, -1.0).reshape(row_count, key_width)
    d_qkv = jnp.concatenate(
        [d_query_rows, d_key_rows, d_values.reshape(row_count, key_width)], axis=1
    ).astype(jnp.bfloat16)
    grad_qkv = jnp.dot(first_in.T, d_qkv, preferred_element_type=jnp.float32)
    d_first = jnp.dot(d_qkv, full_qkv.T, preferred_element_type=jnp.float32)
    d_norm_one = d_first * gain_attn
    grad_attn = jnp.sum(d_first * normed_one, axis=0)
    d_tokens = d_residual + inv_one * (
        d_norm_one - normed_one * jnp.mean(d_norm_one * normed_one, axis=1, keepdims=True)
    )
    share_attn, share_qkv, share_out, share_ffn, share_router = (
        lax.psum_scatter(
            grad_attn.astype(jnp.bfloat16), "shard", scatter_dimension=0, tiled=True
        ).astype(jnp.float32),
        lax.psum_scatter(
            grad_qkv.astype(jnp.bfloat16), "shard", scatter_dimension=0, tiled=True
        ).astype(jnp.float32),
        lax.psum_scatter(
            grad_out.astype(jnp.bfloat16), "shard", scatter_dimension=0, tiled=True
        ).astype(jnp.float32),
        lax.psum_scatter(
            grad_ffn.astype(jnp.bfloat16), "shard", scatter_dimension=0, tiled=True
        ).astype(jnp.float32),
        lax.psum_scatter(
            grad_router.astype(jnp.bfloat16), "shard", scatter_dimension=0, tiled=True
        ).astype(jnp.float32),
    )
    share_attn, share_qkv, share_out, share_ffn, share_router, grad_gate_up, grad_down = (
        lax.psum(share_attn.astype(jnp.bfloat16), "rep").astype(jnp.float32),
        lax.psum(share_qkv.astype(jnp.bfloat16), "rep").astype(jnp.float32),
        lax.psum(share_out.astype(jnp.bfloat16), "rep").astype(jnp.float32),
        lax.psum(share_ffn.astype(jnp.bfloat16), "rep").astype(jnp.float32),
        lax.psum(share_router.astype(jnp.bfloat16), "rep").astype(jnp.float32),
        lax.psum(grad_gate_up.astype(jnp.bfloat16), "rep").astype(jnp.float32),
        lax.psum(grad_down.astype(jnp.bfloat16), "rep").astype(jnp.float32),
    )
    return (
        output,
        d_tokens,
        share_attn,
        share_qkv,
        share_out,
        share_ffn,
        share_router,
        grad_gate_up,
        grad_down,
    )


def solution(mesh):
    return jax.shard_map(
        on_device,
        mesh=mesh,
        in_specs=(
            P(("rep", "shard"), None),
            P(("rep", "shard"), None),
            P("rep", None),
            P("shard"),
            P("shard", None),
            P("shard", None),
            P("shard"),
            P("shard", None),
            P("shard", None, None),
            P("shard", None, None),
            P(("rep", "shard"), None),
        ),
        out_specs=(
            P(("rep", "shard"), None),
            P(("rep", "shard"), None),
            P("shard"),
            P("shard", None),
            P("shard", None),
            P("shard"),
            P("shard", None),
            P("shard", None, None),
            P("shard", None, None),
        ),
        check_vma=False,
    )
```

profile of v0, /device:TPU:0, one launch (start us, length us, event | category | flops | bytes accessed | tf_op | source)
XLA Modules:
  0.0 1476.8 jit_solution(884753934744604636)
XLA Ops:
  8.0 13.5 all-gather
  25.3 34.2 %all-gather.7.cloned.1.call-done = bf16[1024,2048]{1,0:T(8,128)(2,1)} async-done(((bf16[128,2048]{1,0:T(8,128)(2,1)}), bf16[1024,2048]{1,0:T(8,128)(2,1)}) %all-gather.7.cloned.1.call-update) | async-done | bytes 4194320 | tf_op jit(solution)/shard_map/all_gather | solution.py:75
  98.8 39.1 %while.50 = (s32[]{:T(128)}, f32[8,2,256]{2,1,0:T(2,128)S(1)}, f32[8,2,256]{2,1,0:T(2,128)S(1)}, s32[4,512]{1,0:T(4,128)S(1)}, s32[4,512]{1,0:T(4,128)S(1)}, /*i...) while((s32[]{:T(128)}, f32[8,2,256]{2,1,0:T(2,128)S(1)}, ...), condition=%wide.region_8.9_spmd.clone, body=%wide.region_5.8_spmd.clone.sunk | while | flops 285758208 | bytes 18448520 | solution.py:133
  141.1 21.5 %while.51 = (s32[]{:T(128)}, f32[256,8,2,64]{0,3,2,1:T(8,128)}, bf16[4,512,8,64]{1,3,2,0:T(8,128)(2,1)}, s32[4,512]{1,0:T(4,128)S(1)}, s32[4,512]{1,0:T(4,128)S(...) while((s32[]{:T(128)}, f32[256,8,2,64]{0,3,2,1:T(8,128)}, ...), condition=%wide.region_10.11_spmd.clone, body=%wide.region_9.10_spmd.clone.sunk | while | flops 548406016 | bytes 3966091 | solution.py:159
  169.6 13.9 gather_fusion
  183.5 10.1 reshape.538
  206.5 144.7 %all_gather.27 = bf16[1024,32]{0,1:T(8,128)(2,1)S(1)} all-gather(bf16[128,32]{0,1:T(8,128)(2,1)S(1)} %copy-done.45), channel_id=1, replica_groups=mesh['rep'=4,'shard'=8] {'shard'}, dimensions={0}, use_global_device_ids=true | all-gather | bytes 73728 | tf_op jit(solution)/shard_map/all_gather | solution.py:78
  354.8 18.6 %gather_fusion.2 = bf16[3072,1024]{1,0:T(8,128)(2,1)} fusion(bf16[2049,1024]{1,0:T(8,128)(2,1)} %concatenate.40, s32[3072]{0:T(1024)S(1)} %get-tuple-element.744), kind=kCustom, calls=%fused_computation.2 | custom fusion | bytes 12595200 | tf_op jit(solution)/shard_map/gather | solution.py:206
  373.4 10.1 reshape.540
  396.0 13.9 fusion.103
  409.9 125.0 %all-to-all-done.2 = bf16[8,96,4,1024]{3,1,2,0:T(8,128)(2,1)} async-done(((bf16[8,96,4,1024]{3,1,2,0:T(8,128)(2,1)}), bf16[8,96,4,1024]{3,1,2,0:T(8,128)(2,1)}, u32[]{:S(2)}, u32[]{:S(2)}) %all-to-all-start.2) | async-done | bytes 6291488 | tf_op jit(solution)/shard_map/all_to_all | solution.py:207
  535.0 13.2 fusion.94
  561.9 13.0 convert_bitcast_fusion
  581.5 119.4 %all-to-all-done.1 = bf16[8,96,4,1024]{3,1,2,0:T(8,128)(2,1)} async-done(((bf16[8,96,4,1024]{3,1,2,0:T(8,128)(2,1)}), bf16[8,96,4,1024]{3,1,2,0:T(8,128)(2,1)}, u32[]{:S(2)}, u32[]{:S(2)}) %all-to-all-start.1) | async-done | bytes 6291488 | tf_op jit(solution)/shard_map/all_to_all | solution.py:193
  706.2 10.4 copy.150
  716.5 9.7 reshape.539
  726.3 14.5 gather_fusion.1
  747.0 97.6 %all-to-all-done.3 = bf16[8,96,4,1024]{3,1,2,0:T(8,128)(2,1)} async-done(((bf16[8,96,4,1024]{3,1,2,0:T(8,128)(2,1)}), bf16[8,96,4,1024]{3,1,2,0:T(8,128)(2,1)}, u32[]{:S(2)}, u32[]{:S(2)}) %all-to-all-start.3) | async-done | bytes 6291488 | tf_op jit(solution)/shard_map/all_to_all | solution.py:229
  844.6 10.4 copy.155
  855.0 9.7 reshape.541
  864.6 14.8 gather_fusion.3
  889.9 27.5 %while.52 = (s32[]{:T(128)}, f32[8,2,256]{2,1,0:T(2,128)S(1)}, s32[4,512]{1,0:T(4,128)S(1)}, s32[4,512]{1,0:T(4,128)S(1)}, s32[256]{0:T(256)S(1)}, /*index=5*/bf...) while((s32[]{:T(128)}, f32[8,2,256]{2,1,0:T(2,128)S(1)}, ...), condition=%wide.region_27.28_spmd.clone, body=%wide.region_25.27_spmd.clone.sunk | while | flops 549982976 | bytes 19235984 | solution.py:263
  917.4 78.7 %while.53 = (s32[]{:T(128)}, f32[256,8,2,64]{0,3,2,1:T(8,128)S(1)}, bf16[4,512,8,64]{1,3,2,0:T(8,128)(2,1)}, bf16[4,512,8,64]{1,3,2,0:T(8,128)(2,1)}, bf16[4,512...) while((s32[]{:T(128)}, f32[256,8,2,64]{0,3,2,1:T(8,128)S(1)}, ...), condition=%wide.region_29.30_spmd.clone, body=%wide.region_28.29_spmd.clone.sunk | while | flops 1368916736 | bytes 129960704 | solution.py:295
  1009.3 26.7 %reduce-scatter.8.cloned.1.call-done = bf16[256,512]{0,1:T(8,128)(2,1)} async-done(((bf16[2048,512]{0,1:T(8,128)(2,1)}), bf16[256,512]{0,1:T(8,128)(2,1)}) %reduce-scatter.8.cloned.1.call-update) | async-done | bytes 262160 | tf_op jit(solution)/shard_map/reduce_scatter | solution.py:299
  1037.2 36.2 %reduce-scatter.10.cloned.1.call-done = bf16[256,512]{0,1:T(8,128)(2,1)} async-done(((bf16[2048,512]{0,1:T(8,128)(2,1)}), bf16[256,512]{0,1:T(8,128)(2,1)}) %reduce-scatter.10.cloned.1.call-update) | async-done | bytes 262160 | tf_op jit(solution)/shard_map/reduce_scatter | solution.py:302
  1077.9 12.9 bitcast_convert_fusion
  1110.1 51.6 %reduce-scatter.12.cloned.1.call-done = bf16[128,2048]{1,0:T(8,128)(2,1)} async-done(((bf16[1024,2048]{1,0:T(8,128)(2,1)}), bf16[128,2048]{1,0:T(8,128)(2,1)}) %reduce-scatter.12.cloned.1.call-update) | async-done | bytes 524304 | tf_op jit(solution)/shard_map/reduce_scatter | solution.py:326
  1163.6 29.4 %reduce-scatter.16.cloned.1.call-done = bf16[128,32]{1,0:T(8,128)(2,1)} async-done(((bf16[1024,32]{1,0:T(8,128)(2,1)}), bf16[128,32]{1,0:T(8,128)(2,1)}) %reduce-scatter.16.cloned.1.call-update) | async-done | bytes 8208
  1197.6 13.8 all-reduce.4
  1211.6 11.4 all-reduce.5
  1225.8 225.4 %all-reduce.9.cloned.1.call-done = (bf16[128,2048]{1,0:T(8,128)(2,1)}, bf16[128,1024]{1,0:T(8,128)(2,1)}, bf16[4,1024,1024]{2,1,0:T(8,128)(2,1)}, bf16[4,512,1024]{2,1,0:T(8,128)(2,1)}) async-done(((bf16[128,2048]{1,0:T(8,128)(2,1)}, bf16[128,1024]{1,0:T(8,128)(2,1)}, bf16[4,1024,1024]{2,1,0:T(8,128)(2,1)}, bf16[4,512,1024]{2,1,0:T(8,128)(2,1)}), (bf16[128,2048]{1,0:T(8,128)(2,1)}, ...) | async-done | bytes 13369360 | tf_op jit(solution)/shard_map/psum | solution.py:341
  1451.2 11.9 convert_element_type.220
  (379 shorter events, 343.7 us)
Async XLA Ops:
  7.2 52.3 %all-gather.7.cloned.1.call-start = ((), (), s32[]{:S(2)}) async-start(), calls=%async_computation.9 | async-start | bytes 4718592 | tf_op jit(solution)/shard_map/all_gather | solution.py:75
  7.9 89.0 %all-gather.11.cloned.1.call-start = ((), (), s32[]{:S(2)}) async-start(), calls=%async_computation.11 | async-start | bytes 2359296 | tf_op jit(solution)/shard_map/all_gather | solution.py:107
  21.5 44.0 %copy-start.40 = (f32[8,1,128]{2,1,0:T(1,128)}, f32[8,1,128]{2,1,0:T(1,128)S(1)}, u32[]{:S(2)}) copy-start(f32[8,1,128]{2,1,0:T(1,128)S(1)} %convert_element_type.225) | copy-start | bytes 12292
  24.3 41.9 %copy-start.33 = (s32[256,8]{0,1:T(8,128)S(1)}, s32[256,8]{0,1:T(8,128)}, u32[]{:S(2)}) copy-start(s32[256,8]{0,1:T(8,128)} %param.20) | copy-start | bytes 24580
  24.4 38.9 %copy-start.46 = (f32[256]{0:T(256)}, f32[256]{0:T(256)S(1)}, u32[]{:S(2)}) copy-start(f32[256]{0:T(256)S(1)} %add_rsqrt_fusion.1) | copy-start | bytes 3076
  64.6 73.3 %all-gather.9.cloned.1.call-start = ((), (), s32[]{:S(2)}) async-start(), calls=%async_computation.10 | async-start | bytes 2359296 | tf_op jit(solution)/shard_map/all_gather | solution.py:108
  65.5 100.4 %all-gather.13.cloned.1.call-start = ((), (), s32[]{:S(2)}) async-start(), calls=%async_computation.12 | async-start | bytes 2359296 | tf_op jit(solution)/shard_map/all_gather | solution.py:76
  76.3 92.3 %copy-start.34 = (f32[8,1,128]{2,1,0:T(1,128)}, f32[8,1,128]{2,1,0:T(1,128)S(1)}, u32[]{:S(2)}) copy-start(f32[8,1,128]{2,1,0:T(1,128)S(1)} %convert_element_type.226) | copy-start | bytes 12292
  163.8 19.7 %copy-start.22 = (s32[256]{0:T(256)}, s32[256]{0:T(256)S(1)}, u32[]{:S(2)}) copy-start(s32[256]{0:T(256)S(1)} %get-tuple-element.1263) | copy-start | bytes 3076
  163.8 19.7 %copy-start.26 = (s32[4,512]{1,0:T(4,128)}, s32[4,512]{1,0:T(4,128)S(1)}, u32[]{:S(2)}) copy-start(s32[4,512]{1,0:T(4,128)S(1)} %get-tuple-element.1266) | copy-start | bytes 24580
  168.6 14.9 %copy-start.42 = (f32[256]{0:T(256)}, f32[256]{0:T(256)S(1)}, u32[]{:S(2)}) copy-start(f32[256]{0:T(256)S(1)} %add_rsqrt_fusion) | copy-start | bytes 3076
  169.6 181.6 %copy-start.11 = (bf16[256,1024]{1,0:T(8,128)(2,1)}, bf16[256,1024]{1,0:T(8,128)(2,1)S(1)}, u32[]{:S(2)}) copy-start(bf16[256,1024]{1,0:T(8,128)(2,1)S(1)} %multiply_convert_fusion.1) | copy-start | bytes 1572868
  201.5 189.8 %all-to-all-start = ((bf16[8,96,4,1024]{3,1,2,0:T(8,128)(2,1)}), bf16[8,96,4,1024]{3,1,2,0:T(8,128)(2,1)}, u32[]{:S(2)}, u32[]{:S(2)}) async-start(bf16[8,96,4,1024]{3,1,2,0:T(8,128)(2,1)} %copy.147), calls=%async_computation | async-start | bytes 12582912 | tf_op jit(solution)/shard_map/all_to_all | solution.py:187
  391.3 143.7 %all-to-all-start.2 = ((bf16[8,96,4,1024]{3,1,2,0:T(8,128)(2,1)}), bf16[8,96,4,1024]{3,1,2,0:T(8,128)(2,1)}, u32[]{:S(2)}, u32[]{:S(2)}) async-start(bf16[8,96,4,1024]{3,1,2,0:T(8,128)(2,1)} %copy.152), calls=%async_computation.2 | async-start | bytes 12582912 | tf_op jit(solution)/shard_map/all_to_all | solution.py:207
  535.0 13.2 copy-start.49
  557.1 143.7 %all-to-all-start.1 = ((bf16[8,96,4,1024]{3,1,2,0:T(8,128)(2,1)}), bf16[8,96,4,1024]{3,1,2,0:T(8,128)(2,1)}, u32[]{:S(2)}, u32[]{:S(2)}) async-start(bf16[8,96,4,1024]{3,1,2,0:T(8,128)(2,1)} %copy.149), calls=%async_computation.1 | async-start | bytes 12582912 | tf_op jit(solution)/shard_map/all_to_all | solution.py:193
  581.5 124.7 %copy-start.37 = (s32[2048,1]{0,1:T(1,128)S(1)}, s32[2048,1]{0,1:T(1,128)}, u32[]{:S(2)}) copy-start(s32[2048,1]{0,1:T(1,128)} %copy-done.36) | copy-start | bytes 24580
  700.8 143.8 %all-to-all-start.3 = ((bf16[8,96,4,1024]{3,1,2,0:T(8,128)(2,1)}), bf16[8,96,4,1024]{3,1,2,0:T(8,128)(2,1)}, u32[]{:S(2)}, u32[]{:S(2)}) async-start(bf16[8,96,4,1024]{3,1,2,0:T(8,128)(2,1)} %copy.154), calls=%async_computation.3 | async-start | bytes 12582912 | tf_op jit(solution)/shard_map/all_to_all | solution.py:229
  705.6 330.4 %reduce-scatter.8.cloned.1.call-start = ((), (), s32[]{:S(2)}) async-start(), calls=%async_computation.13 | async-start | bytes 2359296 | tf_op jit(solution)/shard_map/reduce_scatter | solution.py:299
  747.0 138.0 %copy-start.24 = (f32[256,32]{0,1:T(8,128)}, f32[256,32]{0,1:T(8,128)S(1)}, u32[]{:S(2)}) copy-start(f32[256,32]{0,1:T(8,128)S(1)} %select_reduce_fusion.1) | copy-start | bytes 98308
  864.6 20.5 %copy-start.7 = (f32[256,1024]{1,0:T(8,128)S(1)}, f32[256,1024]{1,0:T(8,128)}, u32[]{:S(2)}) copy-start(f32[256,1024]{1,0:T(8,128)} %copy-done.6) | copy-start | bytes 3145732
  864.6 20.5 %copy-start.35 = (f32[8,1,128]{2,1,0:T(1,128)S(1)}, f32[8,1,128]{2,1,0:T(1,128)}, u32[]{:S(2)}) copy-start(f32[8,1,128]{2,1,0:T(1,128)} %copy-done.34) | copy-start | bytes 12292
  864.6 20.5 %copy-start.43 = (f32[256]{0:T(256)S(1)}, f32[256]{0:T(256)}, u32[]{:S(2)}) copy-start(f32[256]{0:T(256)} %copy-done.42) | copy-start | bytes 3076
  1001.3 72.1 %reduce-scatter.10.cloned.1.call-start = ((), (), s32[]{:S(2)}) async-start(), calls=%async_computation.14 | async-start | bytes 2359296 | tf_op jit(solution)/shard_map/reduce_scatter | solution.py:302
  1006.6 66.7 %copy-start.15 = (bf16[256,1024]{1,0:T(8,128)(2,1)S(1)}, bf16[256,1024]{1,0:T(8,128)(2,1)}, u32[]{:S(2)}) copy-start(bf16[256,1024]{1,0:T(8,128)(2,1)} %param.19) | copy-start | bytes 1572868
  1006.6 66.7 %copy-start.41 = (f32[8,1,128]{2,1,0:T(1,128)S(1)}, f32[8,1,128]{2,1,0:T(1,128)}, u32[]{:S(2)}) copy-start(f32[8,1,128]{2,1,0:T(1,128)} %copy-done.40) | copy-start | bytes 12292
  1006.6 66.7 %copy-start.47 = (f32[256]{0:T(256)S(1)}, f32[256]{0:T(256)}, u32[]{:S(2)}) copy-start(f32[256]{0:T(256)} %copy-done.46) | copy-start | bytes 3076
  1006.7 103.4 %reduce-scatter.14.cloned.1.call-start = ((), (), s32[]{:S(2)}) async-start(), calls=%async_computation.16 | async-start | bytes 2359296 | tf_op jit(solution)/shard_map/reduce_scatter | solution.py:329
  1008.8 152.9 %reduce-scatter.12.cloned.1.call-start = ((), (), s32[]{:S(2)}) async-start(), calls=%async_computation.15 | async-start | bytes 4718592 | tf_op jit(solution)/shard_map/reduce_scatter | solution.py:326
  1077.8 115.2 %reduce-scatter.16.cloned.1.call-start = ((), (), s32[]{:S(2)}) async-start(), calls=%async_computation.17 | async-start | bytes 294912
  1092.0 359.2 %all-reduce.9.cloned.1.call-start = ((), (), s32[]{:S(2)}) async-start(), calls=%async_computation.18 | async-start | bytes 26738688 | tf_op jit(solution)/shard_map/psum | solution.py:341
  1161.7 35.9 %copy-start.44 = (bf16[1024]{0:T(1024)(128)(2,1)S(1)}, bf16[1024]{0:T(1024)(128)(2,1)}, u32[]{:S(2)}) copy-start(bf16[1024]{0:T(1024)(128)(2,1)} %get-tuple-element.616) | copy-start | bytes 6148
  (42 other events, 210.3 us)
Sparse Core Ops, SparseCore 0:
  9.6 49.8 all-gather.6
  64.7 29.5 all-gather.10
  96.5 29.8 all-gather.8
  127.9 28.1 all-gather.12
  1001.4 34.5 reduce-scatter.7
  1038.8 34.5 reduce-scatter.9
  1075.6 34.4 reduce-scatter.13
  1113.0 48.6 reduce-scatter.11
  1164.5 28.4 reduce-scatter.15
  1198.0 253.2 all-reduce.8
where the time goes:
time: 1480 us
  waiting for transfers between devices  756 us (51%)
  matrix products  215 us (15%)
  local copies, waits for them, and re-layouts  198 us (13%)
  blocking collectives  193 us (13%)
  other arithmetic  76.8 us (5%)
  starting transfers between devices  20.3 us (1%)
  between operations  16.3 us (1%)
    psum x1, waiting for transfers between devices, on_device(): lax.psum(share_qkv.astype(jnp.bfloat16), 'rep').astype(jnp.float32)  225 us
    all_gather x1, blocking collectives, on_device(): lax.all_gather(w_router, 'shard', axis=0, tiled=True)  145 us
    all_to_all x1, waiting for transfers between devices, on_device(): lax.all_to_all(d_send, 'shard', split_axis=0, concat_axis=0, tiled=True)  125 us
    all_to_all x1, waiting for transfers between devices, on_device(): lax.all_to_all(expert_out, 'shard', split_axis=0, concat_axis=0, tiled=True)  119 us
    all_to_all x1, waiting for transfers between devices, on_device(): lax.all_to_all(d_slots, 'shard', split_axis=0, concat_axis=0, tiled=True)  97.6 us
    reduce_scatter x1, waiting for transfers between devices, on_device(): lax.psum_scatter(grad_qkv.astype(jnp.bfloat16), 'shard', scatter_dimensio...  51.6 us
    dot_general x12, matrix products, block_scores(): jnp.einsum('qgrd,kgd->grqk', queries, key_rot, preferred_element_type=jnp...  37.7 us
    reduce_scatter x1, waiting for transfers between devices, on_device(): lax.psum_scatter(value_terms.astype(jnp.bfloat16), 'shard', scatter_dimen...  36.2 us
  transfers between devices with their start and end apart: 14, of which 10 were waited for; matrix products, arithmetic and copies ran while one was open for 17% of the time, Pallas kernels for 0%

commit v1 on v0

--- a/solution.py
+++ b/solution.py
@@ -338,7 +338,7 @@
     )
     share_attn, share_qkv, share_out, share_ffn, share_router, grad_gate_up, grad_down = (
         lax.psum(share_attn.astype(jnp.bfloat16), "rep").astype(jnp.float32),
-        lax.psum(share_qkv.astype(jnp.bfloat16), "rep").astype(jnp.float32),
+        jnp.sum(lax.all_gather(share_qkv.astype(jnp.bfloat16), "rep"), axis=0).astype(jnp.float32),
         lax.psum(share_out.astype(jnp.bfloat16), "rep").astype(jnp.float32),
         lax.psum(share_ffn.astype(jnp.bfloat16), "rep").astype(jnp.float32),
         lax.psum(share_router.astype(jnp.bfloat16), "rep").astype(jnp.float32),

time: 1480 us -> 1550 us (1.047)
  waiting for transfers between devices: 756 us -> 820 us
    all_to_all x1, waiting for transfers between devices: 97.6 us -> 130 us  [on_device(): lax.all_to_all(d_slots, 'shard', split_axis=0, concat_axis=0, tiled=True)]
    all_gather x1, waiting for transfers between devices: 0.02 us -> 24.9 us  [on_device(): lax.all_gather(key_rot, 'shard', axis=0, tiled=True)]
    all_to_all x1, waiting for transfers between devices: 119 us -> 97.5 us  [on_device(): lax.all_to_all(expert_out, 'shard', split_axis=0, concat_axis=0, tiled=True)]
    psum x1, waiting for transfers between devices: 225 us -> 247 us  [on_device(): lax.psum(share_out.astype(jnp.bfloat16), 'rep').astype(jnp.float32)]
    unnamed x11 -> x12, waiting for transfers between devices: 30.7 us -> 31.3 us
  transfers between devices with their start and end apart: 14 -> 15, of which waited for: 10 -> 12; matrix products, arithmetic and copies ran while one was open for 17% -> 15% of each run, Pallas kernels for 0% -> 0%
where the time goes in v1:
time: 1550 us; the launch traced here: 1540 us
  waiting for transfers between devices  820 us (53%)
  matrix products  216 us (14%)
  blocking collectives  193 us (12%)
  local copies, waits for them, and re-layouts  192 us (12%)
  other arithmetic  80.4 us (5%)
  starting transfers between devices  20.5 us (1%)
  between operations  16 us (1%)
    psum x1, waiting for transfers between devices, on_device(): lax.psum(share_out.astype(jnp.bfloat16), 'rep').astype(jnp.float32)  247 us
    all_gather x1, blocking collectives, on_device(): lax.all_gather(w_router, 'shard', axis=0, tiled=True)  145 us
    all_to_all x1, waiting for transfers between devices, on_device(): lax.all_to_all(d_slots, 'shard', split_axis=0, concat_axis=0, tiled=True)  130 us
    all_to_all x1, waiting for transfers between devices, on_device(): lax.all_to_all(d_send, 'shard', split_axis=0, concat_axis=0, tiled=True)  125 us
    all_to_all x1, waiting for transfers between devices, on_device(): lax.all_to_all(expert_out, 'shard', split_axis=0, concat_axis=0, tiled=True)  97.5 us
    reduce_scatter x1, waiting for transfers between devices, on_device(): lax.psum_scatter(grad_qkv.astype(jnp.bfloat16), 'shard', scatter_dimensio...  45.4 us
    dot_general x12, matrix products, block_scores(): jnp.einsum('qgrd,kgd->grqk', queries, key_rot, preferred_element_type=jnp...  37.7 us
    all_gather x1, waiting for transfers between devices, on_device(): lax.all_gather(w_qkv, 'shard', axis=0, tiled=True)  36.7 us
  transfers between devices with their start and end apart: 15, of which 12 were waited for; matrix products, arithmetic and copies ran while one was open for 15% of the time, Pallas kernels for 0%

profile of v1, /device:TPU:0, one launch (start us, length us, event | category | flops | bytes accessed | tf_op | source)
XLA Modules:
  0.0 1539.6 jit_solution(6891443447784329974)
XLA Ops:
  8.0 13.5 all-gather.1
  22.8 36.7 %all-gather.9.cloned.1.call-done = bf16[1024,2048]{1,0:T(8,128)(2,1)} async-done(((bf16[128,2048]{1,0:T(8,128)(2,1)}), bf16[1024,2048]{1,0:T(8,128)(2,1)}) %all-gather.9.cloned.1.call-update) | async-done | bytes 4194320 | tf_op jit(solution)/shard_map/all_gather | solution.py:75
  101.2 24.9 %all-gather.13.cloned.1.call-done = bf16[2048,8,64]{0,2,1:T(8,128)(2,1)} async-done(((bf16[256,8,64]{0,2,1:T(8,128)(2,1)}), bf16[2048,8,64]{0,2,1:T(8,128)(2,1)}) %all-gather.13.cloned.1.call-update) | async-done | bytes 2097168 | tf_op jit(solution)/shard_map/all_gather | solution.py:107
  128.0 38.9 %while.50 = (s32[]{:T(128)}, f32[8,2,256]{2,1,0:T(2,128)S(1)}, f32[8,2,256]{2,1,0:T(2,128)S(1)}, s32[4,512]{1,0:T(4,128)S(1)}, s32[4,512]{1,0:T(4,128)S(1)}, /*i...) while((s32[]{:T(128)}, f32[8,2,256]{2,1,0:T(2,128)S(1)}, ...), condition=%wide.region_8.9_spmd.clone, body=%wide.region_5.8_spmd.clone.sunk | while | flops 285758208 | bytes 18448528 | solution.py:133
  167.0 21.5 %while.51 = (s32[]{:T(128)}, f32[256,8,2,64]{0,3,2,1:T(8,128)}, bf16[4,512,8,64]{1,3,2,0:T(8,128)(2,1)}, s32[4,512]{1,0:T(4,128)S(1)}, s32[4,512]{1,0:T(4,128)S(...) while((s32[]{:T(128)}, f32[256,8,2,64]{0,3,2,1:T(8,128)}, ...), condition=%wide.region_10.11_spmd.clone, body=%wide.region_9.10_spmd.clone.sunk | while | flops 548406016 | bytes 3966610 | solution.py:159
  195.5 13.9 gather_fusion
  209.3 10.1 reshape.538
  232.3 144.6 %all_gather.33 = bf16[1024,32]{0,1:T(8,128)(2,1)S(1)} all-gather(bf16[128,32]{0,1:T(8,128)(2,1)S(1)} %copy-done.43), channel_id=1, replica_groups=mesh['rep'=4,'shard'=8] {'shard'}, dimensions={0}, use_global_device_ids=true | all-gather | bytes 73728 | tf_op jit(solution)/shard_map/all_gather | solution.py:78
  380.7 18.6 %gather_fusion.2 = bf16[3072,1024]{1,0:T(8,128)(2,1)} fusion(bf16[2049,1024]{1,0:T(8,128)(2,1)} %concatenate.40, s32[3072]{0:T(1024)S(1)} %get-tuple-element.743), kind=kCustom, calls=%fused_computation.2 | custom fusion | bytes 12595200 | tf_op jit(solution)/shard_map/gather | solution.py:206
  399.3 10.2 reshape.540
  422.0 13.9 fusion.103
  435.9 125.0 %all-to-all-done.2 = bf16[8,96,4,1024]{3,1,2,0:T(8,128)(2,1)} async-done(((bf16[8,96,4,1024]{3,1,2,0:T(8,128)(2,1)}), bf16[8,96,4,1024]{3,1,2,0:T(8,128)(2,1)}, u32[]{:S(2)}, u32[]{:S(2)}) %all-to-all-start.2) | async-done | bytes 6291488 | tf_op jit(solution)/shard_map/all_to_all | solution.py:207
  560.9 13.0 fusion.94
  574.0 11.3 convert_bitcast_fusion
  602.9 129.7 %all-to-all-done.3 = bf16[8,96,4,1024]{3,1,2,0:T(8,128)(2,1)} async-done(((bf16[8,96,4,1024]{3,1,2,0:T(8,128)(2,1)}), bf16[8,96,4,1024]{3,1,2,0:T(8,128)(2,1)}, u32[]{:S(2)}, u32[]{:S(2)}) %all-to-all-start.3) | async-done | bytes 6291488 | tf_op jit(solution)/shard_map/all_to_all | solution.py:229
  738.0 10.4 copy.155
  758.0 14.5 gather_fusion.3
  778.9 97.5 %all-to-all-done.1 = bf16[8,96,4,1024]{3,1,2,0:T(8,128)(2,1)} async-done(((bf16[8,96,4,1024]{3,1,2,0:T(8,128)(2,1)}), bf16[8,96,4,1024]{3,1,2,0:T(8,128)(2,1)}, u32[]{:S(2)}, u32[]{:S(2)}) %all-to-all-start.1) | async-done | bytes 6291488 | tf_op jit(solution)/shard_map/all_to_all | solution.py:193
  876.4 10.4 copy.150
  896.4 14.5 gather_fusion.1
  925.0 27.5 %while.52 = (s32[]{:T(128)}, f32[8,2,256]{2,1,0:T(2,128)S(1)}, s32[4,512]{1,0:T(4,128)S(1)}, s32[4,512]{1,0:T(4,128)S(1)}, s32[256]{0:T(256)S(1)}, /*index=5*/bf...) while((s32[]{:T(128)}, f32[8,2,256]{2,1,0:T(2,128)S(1)}, ...), condition=%wide.region_27.28_spmd.clone, body=%wide.region_25.27_spmd.clone.sunk | while | flops 549982976 | bytes 19234976 | solution.py:263
  952.5 77.3 %while.53 = (s32[]{:T(128)}, f32[256,8,2,64]{0,3,2,1:T(8,128)S(1)}, bf16[4,512,8,64]{1,3,2,0:T(8,128)(2,1)}, bf16[4,512,8,64]{1,3,2,0:T(8,128)(2,1)}, bf16[4,512...) while((s32[]{:T(128)}, f32[256,8,2,64]{0,3,2,1:T(8,128)S(1)}, ...), condition=%wide.region_29.30_spmd.clone, body=%wide.region_28.29_spmd.clone.sunk | while | flops 1368916736 | bytes 146735440 | solution.py:295
  1040.8 28.8 %reduce-scatter.8.cloned.1.call-done = bf16[256,512]{0,1:T(8,128)(2,1)} async-done(((bf16[2048,512]{0,1:T(8,128)(2,1)}), bf16[256,512]{0,1:T(8,128)(2,1)}) %reduce-scatter.8.cloned.1.call-update) | async-done | bytes 262160 | tf_op jit(solution)/shard_map/reduce_scatter | solution.py:299
  1070.7 36.2 %reduce-scatter.10.cloned.1.call-done = bf16[256,512]{0,1:T(8,128)(2,1)} async-done(((bf16[2048,512]{0,1:T(8,128)(2,1)}), bf16[256,512]{0,1:T(8,128)(2,1)}) %reduce-scatter.10.cloned.1.call-update) | async-done | bytes 262160 | tf_op jit(solution)/shard_map/reduce_scatter | solution.py:302
  1114.8 45.4 %reduce-scatter.12.cloned.1.call-done = bf16[128,2048]{1,0:T(8,128)(2,1)} async-done(((bf16[1024,2048]{1,0:T(8,128)(2,1)}), bf16[128,2048]{1,0:T(8,128)(2,1)}) %reduce-scatter.12.cloned.1.call-update) | async-done | bytes 524304 | tf_op jit(solution)/shard_map/reduce_scatter | solution.py:326
  1169.7 11.9 bitcast_convert_fusion
  1181.6 14.9 reduce-scatter.14.cloned.1.call-done
  1198.4 29.9 %reduce-scatter.16.cloned.1.call-done = bf16[128,32]{1,0:T(8,128)(2,1)} async-done(((bf16[1024,32]{1,0:T(8,128)(2,1)}), bf16[128,32]{1,0:T(8,128)(2,1)}) %reduce-scatter.16.cloned.1.call-update) | async-done | bytes 8208
  1232.9 13.7 all-reduce.4
  1246.9 11.5 all-reduce.5
  1267.3 247.2 %all-reduce.9.cloned.1.call-done = (bf16[128,1024]{1,0:T(8,128)(2,1)}, bf16[4,1024,1024]{2,1,0:T(8,128)(2,1)}, bf16[4,512,1024]{2,1,0:T(8,128)(2,1)}) async-done(((bf16[128,1024]{1,0:T(8,128)(2,1)}, bf16[4,1024,1024]{2,1,0:T(8,128)(2,1)}, bf16[4,512,1024]{2,1,0:T(8,128)(2,1)}), (bf16[128,1024]{1,0:T(8,128)(2,1)}, bf16[4,1024,1024]{2,1,0:T(8,128)(2,1)}, ...) | async-done | bytes 12845072 | tf_op jit(solution)/shard_map/psum | solution.py:342
  1516.3 11.9 convert_element_type.222
  (397 shorter events, 358.3 us)
Async XLA Ops:
  7.2 57.2 %copy-start.47 = (s32[1,2]{1,0:T(1,128)S(1)}, s32[1,2]{1,0:T(1,128)}, u32[]{:S(2)}) copy-start(s32[1,2]{1,0:T(1,128)} %param.21) | copy-start | bytes 28
  7.2 52.3 %all-gather.9.cloned.1.call-start = ((), (), s32[]{:S(2)}) async-start(), calls=%async_computation.9 | async-start | bytes 4718592 | tf_op jit(solution)/shard_map/all_gather | solution.py:75
  7.9 90.1 %all-gather.11.cloned.1.call-start = ((), (), s32[]{:S(2)}) async-start(), calls=%async_computation.10 | async-start | bytes 2359296 | tf_op jit(solution)/shard_map/all_gather | solution.py:108
  21.5 43.0 %copy-start.38 = (f32[8,1,128]{2,1,0:T(1,128)}, f32[8,1,128]{2,1,0:T(1,128)S(1)}, u32[]{:S(2)}) copy-start(f32[8,1,128]{2,1,0:T(1,128)S(1)} %convert_element_type.227) | copy-start | bytes 12292
  22.7 44.7 %copy-start.31 = (s32[256,8]{0,1:T(8,128)S(1)}, s32[256,8]{0,1:T(8,128)}, u32[]{:S(2)}) copy-start(s32[256,8]{0,1:T(8,128)} %param.20) | copy-start | bytes 24580
  22.8 41.9 %copy-start.44 = (f32[256]{0:T(256)}, f32[256]{0:T(256)S(1)}, u32[]{:S(2)}) copy-start(f32[256]{0:T(256)S(1)} %add_rsqrt_fusion.1) | copy-start | bytes 3076
  64.3 61.8 %all-gather.13.cloned.1.call-start = ((), (), s32[]{:S(2)}) async-start(), calls=%async_computation.11 | async-start | bytes 2359296 | tf_op jit(solution)/shard_map/all_gather | solution.py:107
  66.7 125.1 %all-gather.15.cloned.1.call-start = ((), (), s32[]{:S(2)}) async-start(), calls=%async_computation.12 | async-start | bytes 2359296 | tf_op jit(solution)/shard_map/all_gather | solution.py:76
  77.4 117.0 %copy-start.32 = (f32[8,1,128]{2,1,0:T(1,128)}, f32[8,1,128]{2,1,0:T(1,128)S(1)}, u32[]{:S(2)}) copy-start(f32[8,1,128]{2,1,0:T(1,128)S(1)} %convert_element_type.228) | copy-start | bytes 12292
  87.5 40.5 %copy-start.34 = (s32[2048,1]{0,1:T(1,128)}, s32[2048,1]{0,1:T(1,128)S(1)}, u32[]{:S(2)}) copy-start(s32[2048,1]{0,1:T(1,128)S(1)} %compare_select_fusion) | copy-start | bytes 24580
  189.6 19.7 %copy-start.23 = (s32[256]{0:T(256)}, s32[256]{0:T(256)S(1)}, u32[]{:S(2)}) copy-start(s32[256]{0:T(256)S(1)} %get-tuple-element.1262) | copy-start | bytes 3076
  189.7 19.7 %copy-start.25 = (s32[4,512]{1,0:T(4,128)}, s32[4,512]{1,0:T(4,128)S(1)}, u32[]{:S(2)}) copy-start(s32[4,512]{1,0:T(4,128)S(1)} %get-tuple-element.1265) | copy-start | bytes 24580
  195.4 181.6 %copy-start.12 = (bf16[256,1024]{1,0:T(8,128)(2,1)}, bf16[256,1024]{1,0:T(8,128)(2,1)S(1)}, u32[]{:S(2)}) copy-start(bf16[256,1024]{1,0:T(8,128)(2,1)S(1)} %multiply_convert_fusion.1) | copy-start | bytes 1572868
  227.3 189.9 %all-to-all-start = ((bf16[8,96,4,1024]{3,1,2,0:T(8,128)(2,1)}), bf16[8,96,4,1024]{3,1,2,0:T(8,128)(2,1)}, u32[]{:S(2)}, u32[]{:S(2)}) async-start(bf16[8,96,4,1024]{3,1,2,0:T(8,128)(2,1)} %copy.147), calls=%async_computation | async-start | bytes 12582912 | tf_op jit(solution)/shard_map/all_to_all | solution.py:187
  232.3 148.4 %copy-start.10 = (f32[256,1024]{1,0:T(8,128)}, f32[256,1024]{1,0:T(8,128)S(1)}, u32[]{:S(2)}) copy-start(f32[256,1024]{1,0:T(8,128)S(1)} %convert_element_type.199) | copy-start | bytes 3145732
  417.2 143.7 %all-to-all-start.2 = ((bf16[8,96,4,1024]{3,1,2,0:T(8,128)(2,1)}), bf16[8,96,4,1024]{3,1,2,0:T(8,128)(2,1)}, u32[]{:S(2)}, u32[]{:S(2)}) async-start(bf16[8,96,4,1024]{3,1,2,0:T(8,128)(2,1)} %copy.152), calls=%async_computation.2 | async-start | bytes 12582912 | tf_op jit(solution)/shard_map/all_to_all | solution.py:207
  588.7 144.0 %all-to-all-start.3 = ((bf16[8,96,4,1024]{3,1,2,0:T(8,128)(2,1)}), bf16[8,96,4,1024]{3,1,2,0:T(8,128)(2,1)}, u32[]{:S(2)}, u32[]{:S(2)}) async-start(bf16[8,96,4,1024]{3,1,2,0:T(8,128)(2,1)} %copy.154), calls=%async_computation.3 | async-start | bytes 12582912 | tf_op jit(solution)/shard_map/all_to_all | solution.py:229
  602.9 135.0 %copy-start.35 = (s32[2048,1]{0,1:T(1,128)S(1)}, s32[2048,1]{0,1:T(1,128)}, u32[]{:S(2)}) copy-start(s32[2048,1]{0,1:T(1,128)} %copy-done.34) | copy-start | bytes 24580
  732.6 143.8 %all-to-all-start.1 = ((bf16[8,96,4,1024]{3,1,2,0:T(8,128)(2,1)}), bf16[8,96,4,1024]{3,1,2,0:T(8,128)(2,1)}, u32[]{:S(2)}, u32[]{:S(2)}) async-start(bf16[8,96,4,1024]{3,1,2,0:T(8,128)(2,1)} %copy.149), calls=%async_computation.1 | async-start | bytes 12582912 | tf_op jit(solution)/shard_map/all_to_all | solution.py:193
  737.5 332.2 %reduce-scatter.8.cloned.1.call-start = ((), (), s32[]{:S(2)}) async-start(), calls=%async_computation.13 | async-start | bytes 2359296 | tf_op jit(solution)/shard_map/reduce_scatter | solution.py:299
  1035.0 71.9 %reduce-scatter.10.cloned.1.call-start = ((), (), s32[]{:S(2)}) async-start(), calls=%async_computation.14 | async-start | bytes 2359296 | tf_op jit(solution)/shard_map/reduce_scatter | solution.py:302
  1038.3 68.6 %copy-start.16 = (bf16[256,1024]{1,0:T(8,128)(2,1)S(1)}, bf16[256,1024]{1,0:T(8,128)(2,1)}, u32[]{:S(2)}) copy-start(bf16[256,1024]{1,0:T(8,128)(2,1)} %param.19) | copy-start | bytes 1572868
  1038.3 68.6 %copy-start.39 = (f32[8,1,128]{2,1,0:T(1,128)S(1)}, f32[8,1,128]{2,1,0:T(1,128)}, u32[]{:S(2)}) copy-start(f32[8,1,128]{2,1,0:T(1,128)} %copy-done.38) | copy-start | bytes 12292
  1038.3 68.6 %copy-start.45 = (f32[256]{0:T(256)S(1)}, f32[256]{0:T(256)}, u32[]{:S(2)}) copy-start(f32[256]{0:T(256)} %copy-done.44) | copy-start | bytes 3076
  1040.3 119.9 %reduce-scatter.12.cloned.1.call-start = ((), (), s32[]{:S(2)}) async-start(), calls=%async_computation.15 | async-start | bytes 4718592 | tf_op jit(solution)/shard_map/reduce_scatter | solution.py:326
  1070.6 40.8 %copy-start.9 = (f32[256,1024]{1,0:T(8,128)S(1)}, f32[256,1024]{1,0:T(8,128)}, u32[]{:S(2)}) copy-start(f32[256,1024]{1,0:T(8,128)} %copy-done.8) | copy-start | bytes 3145732
  1070.6 40.8 %copy-start.15 = (bf16[256,8,2,64]{0,3,2,1:T(8,128)(2,1)S(1)}, bf16[256,8,2,64]{0,3,2,1:T(8,128)(2,1)}, u32[]{:S(2)}) copy-start(bf16[256,8,2,64]{0,3,2,1:T(8,128)(2,1)} %copy-done.14) | copy-start | bytes 1572868
  1111.4 85.1 %reduce-scatter.14.cloned.1.call-start = ((), (), s32[]{:S(2)}) async-start(), calls=%async_computation.16 | async-start | bytes 2359296 | tf_op jit(solution)/shard_map/reduce_scatter | solution.py:329
  1113.5 114.8 %reduce-scatter.16.cloned.1.call-start = ((), (), s32[]{:S(2)}) async-start(), calls=%async_computation.18 | async-start | bytes 294912
  1114.8 149.4 %all-gather.17.cloned.1.call-start = ((), (), s32[]{:S(2)}) async-start(), calls=%async_computation.17 | async-start | bytes 2621440 | tf_op jit(solution)/shard_map/all_gather | solution.py:341
  1160.2 354.2 %all-reduce.9.cloned.1.call-start = ((), (), s32[]{:S(2)}) async-start(), calls=%async_computation.19 | async-start | bytes 25690112 | tf_op jit(solution)/shard_map/psum | solution.py:342
  1196.5 36.4 %copy-start.42 = (bf16[1024]{0:T(1024)(128)(2,1)S(1)}, bf16[1024]{0:T(1024)(128)(2,1)}, u32[]{:S(2)}) copy-start(bf16[1024]{0:T(1024)(128)(2,1)} %get-tuple-element.616) | copy-start | bytes 6148
  (50 other events, 272.7 us)
Sparse Core Ops, SparseCore 0:
  9.6 49.8 all-gather.8
  64.4 29.5 all-gather.10
  96.2 29.8 all-gather.12
  127.6 28.1 all-gather.14
  1035.1 34.4 reduce-scatter.7
  1072.3 34.5 reduce-scatter.9
  1111.5 48.6 reduce-scatter.11
  1162.5 33.9 reduce-scatter.13
  1199.3 28.9 reduce-scatter.15
  1230.1 33.9 all-gather.16
  1269.8 244.6 all-reduce.8
